TPU v7x, 256 devices: a whole 4x4x8 slice. The times are simulated.
256 devices in a mesh: tm: 8 (over x, y_lo), pts: 32 (over y_hi, z, core).
Axes of the slice: x: 4, y: 4 (y_hi: 2, y_lo: 2; y = y_hi * 2 + y_lo), z: 8, core: 2. Of those that a mesh axis runs over, the one named last changes fastest.
Arguments:
- orbitals: bfloat16 [32768, 2048], P('pts'), may hold values from -6 to 6
- panel_orbitals: bfloat16 [1024, 2048], P(('tm', 'pts')), may hold values from -0.1796875 to 0.1796875
- band_gap: float32 [2048], replicated, may hold values from 0.1 to 1
- tau_points: float32 [8], replicated, may hold values from 0.1 to 2
- quad_weight: float32 [8], replicated, may hold values from 0.1 to 1
- frequencies: float32 [8], replicated, may hold values from 0.1 to 3
- coulomb: bfloat16 [1024, 1024], P(('tm', 'pts')), may hold values from -0.1875 to 0.1875
Outputs:
- screened: bfloat16 [8, 32768, 1024], P(None, ('pts', 'tm'))
All inputs are finite; a program needn't handle non-finite values.
Results may differ from a plain program's by a relative error of at most 0.0056.
Values may be sent and summed in bfloat16 or wider, within the bound.
No kernel may reach another device: no remote copies, remote signals or barrier semaphores. Data moves between devices by JAX's collectives and lax.ppermute only.
A program may use at most 64 MiB of HBM per device.

v0:
```python
import jax
import jax.numpy as jnp
from jax import lax
from jax.sharding import PartitionSpec as P

NOCC = 512
PANEL = 1024
TAU_DEV = 1
FREQS = 8


def laid_out(pieces, dim):
    lengths = list(pieces.shape[1:])
    lengths[dim] *= pieces.shape[0]
    return jnp.moveaxis(pieces, 0, dim).reshape(lengths)


def sent_to_all(value, axis):
    copies = jnp.broadcast_to(value, (lax.axis_size(axis), *value.shape))
    return lax.all_to_all(copies, axis, split_axis=0, concat_axis=0, tiled=True)


def gather_directly(value, axis, dim):
    return laid_out(sent_to_all(value, axis), dim)


def in_blocks(value, dim, devices):
    before, after = (value.shape[:dim], value.shape[dim + 1 :])
    return jnp.moveaxis(value.reshape(*before, devices, -1, *after), dim, 0)


def cut_rows(length, count):
    lap = length // count
    if lap >= 8:
        lap -= lap % 8
    return [lap * k for k in range(1, count)]


def several_exchanges(value, axis, pieces, split_dim, concat_dim):
    blocks = in_blocks(value, split_dim, lax.axis_size(axis))
    cut = max(range(1, max(2, blocks.ndim - 1)), key=lambda d: blocks.shape[d])
    gathered = []
    for section in jnp.split(blocks, cut_rows(blocks.shape[cut], pieces), axis=cut):
        if section.size:
            gathered.append(lax.all_to_all(section, axis, split_axis=0, concat_axis=0, tiled=True))
    return laid_out(jnp.concatenate(gathered, axis=cut), concat_dim)


def contract(left, right):
    return lax.dot_general(
        left, right, (((1,), (1,)), ((), ())), preferred_element_type=jnp.float32
    )


def shards(orbitals, panel_orbitals, band_gap, tau_points, quad_weight, frequencies, coulomb):
    group = lax.axis_index("tm")
    own_taus = lax.dynamic_slice_in_dim(tau_points, group * TAU_DEV, TAU_DEV)
    decay = jnp.exp(-band_gap[None, :] * own_taus[:, None])
    occ_rows = orbitals[:, :NOCC]
    vir_rows = orbitals[:, NOCC:]
    grouped = gather_directly(panel_orbitals, "pts", 0)
    widened = lax.all_gather(grouped, "tm", axis=0, tiled=True).astype(jnp.float32)
    scaled = (widened * decay[0][None, :]).astype(jnp.bfloat16)
    green_occ = contract(occ_rows, scaled[:, :NOCC])
    green_vir = contract(vir_rows, scaled[:, NOCC:])
    layers = [(-(green_occ * green_vir)).astype(jnp.bfloat16)]
    polar = jnp.stack(layers)
    regrouped = several_exchanges(polar, "tm", 2, 1, 0)
    times_all = regrouped.shape[0]
    row_count = regrouped.shape[1]
    cosines = quad_weight[None, :] * jnp.cos(frequencies[:, None] * tau_points[None, :])
    flat = regrouped.reshape(times_all, row_count * PANEL).astype(jnp.float32)
    transformed = jnp.dot(cosines, flat, precision=lax.Precision.HIGHEST).astype(jnp.bfloat16)
    transformed = transformed.reshape(FREQS * row_count, PANEL)
    screened = jnp.dot(
        transformed,
        lax.all_gather(coulomb, ("tm", "pts"), axis=0, tiled=True),
        preferred_element_type=jnp.float32,
    )
    return screened.astype(jnp.bfloat16).reshape(FREQS, row_count, PANEL)


def solution(mesh):
    placed = (P("pts", None), P(("tm", "pts"), None), P(), P(), P(), P(), P(("tm", "pts"), None))
    return jax.shard_map(
        shards, mesh=mesh, in_specs=placed, out_specs=P(None, ("pts", "tm"), None), check_vma=False
    )
```

profile of v0, /device:TPU:98, one launch (start us, length us, event | category | flops | bytes accessed | tf_op | source)
XLA Modules:
  0.0 566.2 jit_solution(4525019650464051369)
XLA Ops:
  6.5 0.0 copy-start.2
  6.5 0.0 all-gather.4.cloned.1.call-start
  6.5 1.0 broadcast_in_dim.2
  7.5 27.3 %all_to_all.15 = bf16[32,4,2048]{2,1,0:T(4,128)(2,1)S(1)} all-to-all(bf16[32,4,2048]{2,1,0:T(4,128)(2,1)S(1)} %broadcast_in_dim.2), channel_id=1, replica_groups=mesh['tm'=8,'pts'=32] {'pts'}, dimensions={0} | all-to-all | bytes 1048576 | tf_op jit(solution)/shard_map/all_to_all | solution.py:20
  34.9 0.9 reshape.19
  35.8 0.0 all-gather.4.cloned.1.call-update
  35.8 0.0 all-gather.6.cloned.1.call-start
  35.8 0.7 all-gather.6.cloned.1.call-update
  36.5 0.0 copy-done.2
  36.6 0.7 dynamic_slice.3
  37.2 0.0 copy-done.1
  37.2 0.7 multiply_exponential_fusion
  37.9 87.4 %all-gather.4.cloned.1.call-done = bf16[1024,2048]{1,0:T(8,128)(2,1)} async-done(((bf16[128,2048]{1,0:T(8,128)(2,1)}), bf16[1024,2048]{1,0:T(8,128)(2,1)}) %all-gather.4.cloned.1.call-update) | async-done | bytes 4194320 | tf_op jit(solution)/shard_map/all_gather | solution.py:62
  125.4 3.4 multiply_convert_fusion
  128.8 0.0 copy-done
  128.8 3.4 fusion
  132.3 1.3 negate_convert_fusion
  133.6 1.2 fusion.11
  134.8 20.0 %all_to_all.16 = bf16[8,1,64,1024]{3,2,1,0:T(8,128)(2,1)S(1)} all-to-all(bf16[8,1,64,1024]{3,2,1,0:T(8,128)(2,1)S(1)} %get-tuple-element.5), channel_id=1, replica_groups=mesh['tm'=8,'pts'=32] {'tm'}, dimensions={0} | all-to-all | bytes 2097152 | tf_op jit(solution)/shard_map/all_to_all | solution.py:45
  154.8 4.8 all-to-all-start.2
  159.6 384.3 %all-gather.6.cloned.1.call-done = bf16[256,4,1024]{2,1,0:T(4,128)(2,1)} async-done(((bf16[1,4,1024]{2,1,0:T(4,128)(2,1)}), bf16[256,4,1024]{2,1,0:T(4,128)(2,1)}) %all-gather.6.cloned.1.call-update) | async-done | bytes 2097168 | tf_op jit(solution)/shard_map/all_gather | solution.py:77
  543.9 4.0 reshape.23
  547.9 0.0 all-to-all-done.2
  547.9 0.2 maximum_bitcast_fusion
  548.1 0.0 copy-start.3
  548.1 0.0 copy-start.4
  548.1 1.2 copy.10
  549.3 0.0 copy-done.3
  549.3 0.0 copy-done.4
  549.3 1.9 convolution_convert_fusion
  551.2 2.3 reshape.20
  553.5 5.9 %convolution_convert_fusion.1 = bf16[1024,1024]{1,0:T(8,128)(2,1)} fusion(bf16[1024,1024]{1,0:T(8,128)(2,1)} %reshape.20, bf16[1024,1024]{1,0:T(8,128)(2,1)} %reshape.23), kind=kOutput, calls=%fused_computation.7 | convolution fusion | flops 2148532224 | bytes 6291456 | tf_op jit(solution)/shard_map/dot_general | solution.py:75
  (2 shorter events, 0.0 us)
Async XLA Ops:
  6.5 30.0 %copy-start.2 = (f32[8]{0:T(128)S(1)}, f32[8]{0:T(128)}, u32[]{:S(2)}) copy-start(f32[8]{0:T(128)} %param.10) | copy-start | bytes 100
  6.5 30.7 %copy-start.1 = (f32[2048]{0:T(1024)S(1)}, f32[2048]{0:T(1024)}, u32[]{:S(2)}) copy-start(f32[2048]{0:T(1024)} %param.9) | copy-start | bytes 24580
  6.5 118.8 %all-gather.4.cloned.1.call-start = ((), (), s32[]{:S(2)}) async-start(), calls=%async_computation.3 | async-start | bytes 4718592 | tf_op jit(solution)/shard_map/all_gather | solution.py:62
  35.8 508.1 %all-gather.6.cloned.1.call-start = ((), (), s32[]{:S(2)}) async-start(), calls=%async_computation.4 | async-start | bytes 2105344 | tf_op jit(solution)/shard_map/all_gather | solution.py:77
  125.4 3.5 copy-start
  154.8 393.1 %all-to-all-start.2 = ((bf16[8,1,64,1024]{3,2,1,0:T(8,128)(2,1)}), bf16[8,1,64,1024]{3,2,1,0:T(8,128)(2,1)S(1)}, u32[]{:S(2)}, u32[]{:S(2)}) async-start(bf16[8,1,64,1024]{3,2,1,0:T(8,128)(2,1)} %get-tuple-element.6), calls=%async_computation.2 | async-start | bytes 2097152 | tf_op jit(solution)/shard_map/all_to_all | solution.py:45
  548.1 1.2 copy-start.3
  548.1 1.2 copy-start.4
Sparse Core Ops, SparseCore 0:
  35.9 89.4 all-gather.3
  127.3 416.5 all-gather.5
where the time goes:
time: 567 us; the launch traced here: 566 us
  waiting for transfers between devices  472 us (83%)
  blocking collectives  47.4 us (8%)
  between operations  13.5 us (2%)
  matrix products  12.5 us (2%)
  local copies, waits for them, and re-layouts  11.1 us (2%)
    all_gather x1, waiting for transfers between devices, shards(): lax.all_gather(coulomb, ('tm', 'pts'), axis=0, tiled=True)  384 us
    all_gather x1, waiting for transfers between devices, shards(): lax.all_gather(grouped, 'tm', axis=0, tiled=True).astype(jnp.float32)  87.4 us
    all_to_all x1, blocking collectives, sent_to_all(): return lax.all_to_all(copies, axis, split_axis=0, concat_axis=0, tiled=True)  27.3 us
    all_to_all x1, blocking collectives, several_exchanges(): lax.all_to_all(section, axis, split_axis=0, concat_axis=0, tiled=True)  20 us
  transfers between devices with their start and end apart: 3, of which 2 were waited for; matrix products, arithmetic and copies ran while one was open for 3% of the time, Pallas kernels for 0%

commit v1 on v0

--- a/solution.py
+++ b/solution.py
@@ -59,7 +59,9 @@
     occ_rows = orbitals[:, :NOCC]
     vir_rows = orbitals[:, NOCC:]
     grouped = gather_directly(panel_orbitals, "pts", 0)
-    widened = lax.all_gather(grouped, "tm", axis=0, tiled=True).astype(jnp.float32)
+    widened = jnp.concatenate(
+        lax.all_to_all(jnp.stack([grouped] * lax.axis_size("tm")), "tm", 0, 0), axis=0
+    ).astype(jnp.float32)
     scaled = (widened * decay[0][None, :]).astype(jnp.bfloat16)
     green_occ = contract(occ_rows, scaled[:, :NOCC])
     green_vir = contract(vir_rows, scaled[:, NOCC:])

time: 567 us -> 507 us (0.89)
  waiting for transfers between devices: 472 us -> 407 us
    all_gather x1 -> x0, waiting for transfers between devices: 87.4 us -> none  [shards(): lax.all_gather(grouped, 'tm', axis=0, tiled=True).astype(jnp.float32)]
    all_to_all x0 -> x1, waiting for transfers between devices: none -> 54.8 us  [shards(): lax.all_to_all(jnp.stack([grouped] * lax.axis_size('tm')), 'tm', 0, 0)]
    all_gather x1, waiting for transfers between devices: 384 us -> 352 us  [shards(): lax.all_gather(coulomb, ('tm', 'pts'), axis=0, tiled=True)]
where the time goes in v1:
time: 507 us; the launch traced here: 506 us
  waiting for transfers between devices  407 us (80%)
  blocking collectives  45.9 us (9%)
  between operations  13.5 us (3%)
  local copies, waits for them, and re-layouts  12.8 us (3%)
  matrix products  12.5 us (2%)
  starting transfers between devices  10 us (2%)
    all_gather x1, waiting for transfers between devices, shards(): lax.all_gather(coulomb, ('tm', 'pts'), axis=0, tiled=True)  352 us
    all_to_all x1, waiting for transfers between devices, shards(): lax.all_to_all(jnp.stack([grouped] * lax.axis_size('tm')), 'tm', 0, 0)  54.8 us
    all_to_all x1, blocking collectives, sent_to_all(): return lax.all_to_all(copies, axis, split_axis=0, concat_axis=0, tiled=True)  27.3 us
    all_to_all x1, blocking collectives, several_exchanges(): lax.all_to_all(section, axis, split_axis=0, concat_axis=0, tiled=True)  18.5 us
  transfers between devices with their start and end apart: 3, of which 2 were waited for; matrix products, arithmetic and copies ran while one was open for 3% of the time, Pallas kernels for 0%

profile of v1, /device:TPU:98, one launch (start us, length us, event | category | flops | bytes accessed | tf_op | source)
XLA Modules:
  0.0 506.4 jit_solution(2199915234871344978)
XLA Ops:
  6.5 0.9 broadcast_in_dim.2
  7.5 27.3 %all_to_all.20 = bf16[32,4,2048]{2,1,0:T(4,128)(2,1)S(1)} all-to-all(bf16[32,4,2048]{2,1,0:T(4,128)(2,1)S(1)} %broadcast_in_dim.2), channel_id=1, replica_groups=mesh['tm'=8,'pts'=32] {'pts'}, dimensions={0} | all-to-all | bytes 1048576 | tf_op jit(solution)/shard_map/all_to_all | solution.py:20
  34.8 0.1 stack_reshape.2
  34.9 2.5 stack.3
  37.5 0.0 copy-start.2
  37.5 0.0 copy-start.1
  37.5 5.1 %all-to-all-start.1 = ((bf16[8,128,2048]{2,1,0:T(8,128)(2,1)}), bf16[8,128,2048]{2,1,0:T(8,128)(2,1)}, u32[]{:S(2)}, u32[]{:S(2)}) async-start(bf16[8,128,2048]{2,1,0:T(8,128)(2,1)} %stack.3), calls=%async_computation.1 | async-start | bytes 8388608 | tf_op jit(solution)/shard_map/all_to_all | solution.py:63
  42.6 0.0 all-gather.3.cloned.1.call-start
  42.6 0.7 all-gather.3.cloned.1.call-update
  43.3 0.0 copy-done.2
  43.3 0.6 dynamic_slice.3
  43.9 0.0 copy-done.1
  43.9 0.7 multiply_exponential_fusion
  44.6 54.8 %all-to-all-done.1 = bf16[8,128,2048]{2,1,0:T(8,128)(2,1)} async-done(((bf16[8,128,2048]{2,1,0:T(8,128)(2,1)}), bf16[8,128,2048]{2,1,0:T(8,128)(2,1)}, u32[]{:S(2)}, u32[]{:S(2)}) %all-to-all-start.1) | async-done | bytes 4194336 | tf_op jit(solution)/shard_map/all_to_all | solution.py:63
  99.4 0.0 copy-start
  99.4 3.4 fusion
  102.8 0.0 copy-done
  102.8 3.5 fusion.1
  106.3 1.3 negate_convert_fusion
  107.6 1.2 fusion.12
  108.8 18.5 %all_to_all.21 = bf16[8,1,64,1024]{3,2,1,0:T(8,128)(2,1)S(1)} all-to-all(bf16[8,1,64,1024]{3,2,1,0:T(8,128)(2,1)S(1)} %get-tuple-element.5), channel_id=1, replica_groups=mesh['tm'=8,'pts'=32] {'tm'}, dimensions={0} | all-to-all | bytes 2097152 | tf_op jit(solution)/shard_map/all_to_all | solution.py:45
  127.3 4.9 all-to-all-start.3
  132.3 351.9 %all-gather.3.cloned.1.call-done = bf16[256,4,1024]{2,1,0:T(4,128)(2,1)} async-done(((bf16[1,4,1024]{2,1,0:T(4,128)(2,1)}), bf16[256,4,1024]{2,1,0:T(4,128)(2,1)}) %all-gather.3.cloned.1.call-update) | async-done | bytes 2097168 | tf_op jit(solution)/shard_map/all_gather | solution.py:79
  484.1 4.0 reshape.25
  488.1 0.0 all-to-all-done.3
  488.1 0.2 maximum_bitcast_fusion
  488.4 1.2 copy.10
  489.5 0.0 copy-done.3
  489.5 0.0 copy-done.4
  489.5 1.9 convolution_convert_fusion
  491.4 2.3 reshape.21
  493.7 5.9 %convolution_convert_fusion.1 = bf16[1024,1024]{1,0:T(8,128)(2,1)} fusion(bf16[1024,1024]{1,0:T(8,128)(2,1)} %reshape.21, bf16[1024,1024]{1,0:T(8,128)(2,1)} %reshape.25), kind=kOutput, calls=%fused_computation.8 | convolution fusion | flops 2148532224 | bytes 6291456 | tf_op jit(solution)/shard_map/dot_general | solution.py:77
  (2 shorter events, 0.0 us)
Async XLA Ops:
  37.5 5.8 %copy-start.2 = (f32[8]{0:T(128)S(1)}, f32[8]{0:T(128)}, u32[]{:S(2)}) copy-start(f32[8]{0:T(128)} %param.10) | copy-start | bytes 100
  37.5 6.4 %copy-start.1 = (f32[2048]{0:T(1024)S(1)}, f32[2048]{0:T(1024)}, u32[]{:S(2)}) copy-start(f32[2048]{0:T(1024)} %param.9) | copy-start | bytes 24580
  37.5 61.9 %all-to-all-start.1 = ((bf16[8,128,2048]{2,1,0:T(8,128)(2,1)}), bf16[8,128,2048]{2,1,0:T(8,128)(2,1)}, u32[]{:S(2)}, u32[]{:S(2)}) async-start(bf16[8,128,2048]{2,1,0:T(8,128)(2,1)} %stack.3), calls=%async_computation.1 | async-start | bytes 8388608 | tf_op jit(solution)/shard_map/all_to_all | solution.py:63
  42.6 441.6 %all-gather.3.cloned.1.call-start = ((), (), s32[]{:S(2)}) async-start(), calls=%async_computation.4 | async-start | bytes 2105344 | tf_op jit(solution)/shard_map/all_gather | solution.py:79
  99.4 3.5 copy-start
  127.3 360.8 %all-to-all-start.3 = ((bf16[8,1,64,1024]{3,2,1,0:T(8,128)(2,1)}), bf16[8,1,64,1024]{3,2,1,0:T(8,128)(2,1)S(1)}, u32[]{:S(2)}, u32[]{:S(2)}) async-start(bf16[8,1,64,1024]{3,2,1,0:T(8,128)(2,1)} %get-tuple-element.6), calls=%async_computation.3 | async-start | bytes 2097152 | tf_op jit(solution)/shard_map/all_to_all | solution.py:45
  488.1 1.4 copy-start.3
  488.1 1.4 copy-start.4
Sparse Core Ops, SparseCore 0:
  45.3 438.8 all-gather.2
